TPU v7x, 128 devices: a whole 4x4x4 slice. The times are simulated.
128 devices in a mesh: dp: 8 (over x, core), ctx: 4 (over y), tensor: 4 (over z).
Axes of the slice: x: 4, y: 4, z: 4, core: 2. Of those that a mesh axis runs over, the one named last changes fastest.
Arguments:
- hidden: bfloat16 [8, 16384, 2560], P('dp', 'ctx', 'tensor'), may hold values from -6 to 6
- depth: int32 [8, 16384], P('dp', 'ctx'), may hold values from 1 to 4, as said below
- qkv_weight: bfloat16 [2560, 3, 2560], P(None, None, 'tensor'), may hold values from -0.125 to 0.125
- out_weight: bfloat16 [2560, 2560], P('tensor'), may hold values from -0.125 to 0.125
Outputs:
- update: bfloat16 [8, 16384, 2560], P('dp', 'ctx', 'tensor')
Inputs may be any that keep to these rules, and one draw needn't show every extreme that they name: In every aligned block of 4096 positions of a document at most 1024 tokens have depth at least 3, and some block has exactly 1024; over all documents exactly 16384 tokens do.
All inputs are finite; a program needn't handle non-finite values.
Results may differ from a plain program's by a relative error of at most 0.012.
The roundings to bfloat16 on the way count: a program that leaves them out, or rounds other values in their place, can miss the bound.
Values may be sent and summed in bfloat16 or wider, within the bound.
No kernel may reach another device: no remote copies, remote signals or barrier semaphores. Data moves between devices by JAX's collectives and lax.ppermute only.
A program may use at most 256 MiB of HBM per device.

v0:
```python
import jax
import jax.numpy as jnp
from jax import lax
from jax.sharding import PartitionSpec as P

HD = 128
RECURSION = 3
ACT_DEV = 512
CAP = 1024
score_scale = 0.25
norm_epsilon = 1e-05
head_epsilon = 1e-06


def head_normed(values):
    row_count = values.shape[0]
    per_head = values.reshape(row_count, -1, HD)
    factor = lax.rsqrt(jnp.mean(per_head * per_head, axis=2, keepdims=True) + head_epsilon)
    return (per_head * factor).reshape(row_count, -1).astype(jnp.bfloat16)


def project_rows(token_rows, qkv_weight):
    full_rows = lax.all_gather(token_rows, "tensor", axis=1, tiled=True)
    widened = full_rows.astype(jnp.float32)
    factor = lax.rsqrt(jnp.mean(widened * widened, axis=1, keepdims=True) + norm_epsilon)
    normed = (widened * factor).astype(jnp.bfloat16)
    head_width = qkv_weight.shape[2]
    projection = jnp.dot(
        normed,
        qkv_weight.reshape(qkv_weight.shape[0], 3 * head_width),
        preferred_element_type=jnp.float32,
    )
    queries = head_normed(projection[:, :head_width])
    keys_normed = head_normed(projection[:, head_width : 2 * head_width])
    values_out = projection[:, 2 * head_width :].astype(jnp.bfloat16)
    return jnp.concatenate([queries, keys_normed, values_out], axis=1)


def output_rows(context, out_weight):
    partial_value = jnp.dot(context, out_weight, preferred_element_type=jnp.float32)
    return lax.psum_scatter(
        partial_value.astype(jnp.bfloat16), "tensor", scatter_dimension=1, tiled=True
    )


def move_tiles(payload):
    return lax.all_to_all(payload, ("dp", "ctx"), split_axis=0, concat_axis=0, tiled=True)


def per_device(hidden, depth, qkv_weight, out_weight):
    tokens = hidden[0]
    local_len = tokens.shape[0]
    feature_width = tokens.shape[1]
    capacity = CAP
    head_width = out_weight.shape[0]
    heads_here = head_width // HD
    ctx_count = lax.axis_size("ctx")
    spread_size = lax.axis_size("dp") * ctx_count
    ctx_rank = lax.axis_index("ctx")
    my_index = lax.axis_index("dp") * ctx_count + ctx_rank
    active = (depth[0] >= RECURSION).astype(jnp.int32)
    active_count = jnp.sum(active)
    active_rank = jnp.cumsum(active) - 1
    slot_token = (
        jnp.zeros((capacity,), jnp.int32)
        .at[jnp.where(active > 0, active_rank, capacity)]
        .set(jnp.arange(local_len, dtype=jnp.int32), mode="drop")
    )
    filled = jnp.arange(capacity, dtype=jnp.int32) < active_count
    token_rows = jnp.where(filled[:, None], tokens[slot_token], jnp.zeros((), tokens.dtype))
    counts = lax.all_gather(active_count[None], ("dp", "ctx"), axis=0, tiled=True)
    doc_counts = lax.dynamic_slice_in_dim(counts, lax.axis_index("dp") * ctx_count, ctx_count)
    slot_size = capacity // spread_size
    offsets = jnp.cumsum(counts) - counts
    first_rank = offsets[my_index]
    global_rank = first_rank + jnp.arange(capacity, dtype=jnp.int32)
    target = global_rank % spread_size
    position = (
        global_rank // spread_size
        - first_rank // spread_size
        - (target < first_rank % spread_size).astype(jnp.int32)
    )
    send_at = jnp.where(filled, target * slot_size + position, capacity)
    fetch_at = jnp.minimum(send_at, capacity - 1)
    lower_bound = (offsets - my_index + spread_size - 1) // spread_size
    upper_bound = (offsets + counts - my_index + spread_size - 1) // spread_size
    arrived = (
        jnp.arange(slot_size, dtype=jnp.int32)[None, :] < (upper_bound - lower_bound)[:, None]
    ).reshape(-1)
    arrived_rank = jnp.cumsum(arrived.astype(jnp.int32)) - 1
    chosen = (
        jnp.zeros((ACT_DEV,), jnp.int32)
        .at[jnp.where(arrived, arrived_rank, ACT_DEV)]
        .set(jnp.arange(capacity, dtype=jnp.int32), mode="drop")
    )
    packed = (
        jnp.zeros((capacity,) + token_rows.shape[1:], token_rows.dtype)
        .at[send_at]
        .set(token_rows, mode="drop")
    )
    values = project_rows(move_tiles(packed)[chosen], qkv_weight)
    bring_packed = jnp.zeros((capacity,) + values.shape[1:], values.dtype).at[chosen].set(values)
    projected = move_tiles(bring_packed)[fetch_at]
    queries = projected[:, :head_width]
    key_values = projected[:, head_width:]
    query_heads = queries.reshape(capacity, heads_here, HD)
    key_piece = lax.all_gather(key_values, "ctx", axis=0, tiled=True)
    piece_rows = key_piece.shape[0]
    row_index = jnp.arange(piece_rows, dtype=jnp.int32)
    source_shard = row_index // capacity
    source_slot = row_index - source_shard * capacity
    clipped = jnp.clip(source_shard, 0, ctx_count - 1)
    key_filled = (source_shard >= 0) & (source_slot < doc_counts[clipped])
    same_block = (source_shard == ctx_rank)[None, :] & (
        slot_token[source_slot][None, :] <= slot_token[:, None]
    )
    earlier = (source_shard < ctx_rank)[None, :] | same_block
    allowed = earlier & key_filled[None, :] & filled[:, None]
    key_heads = key_piece[:, :head_width].reshape(piece_rows, heads_here, HD)
    value_heads = key_piece[:, head_width:].reshape(piece_rows, heads_here, HD)
    scores = (
        jnp.einsum("qhd,khd->hqk", query_heads, key_heads, preferred_element_type=jnp.float32)
        * score_scale
    )
    weights = jnp.where(allowed[None], jnp.exp(scores), 0.0)
    numerator = jnp.einsum(
        "hqk,khd->qhd",
        weights.astype(jnp.bfloat16),
        value_heads,
        preferred_element_type=jnp.float32,
    )
    denominator = jnp.sum(weights, axis=2)
    numerator, denominator = (numerator, denominator)
    guarded = denominator + (1.0 - filled.astype(jnp.float32))[None, :]
    context = (
        (numerator / jnp.transpose(guarded)[:, :, None])
        .reshape(capacity, head_width)
        .astype(jnp.bfloat16)
    )
    result_rows = output_rows(context, out_weight)
    update = (
        jnp.zeros((local_len, feature_width), jnp.bfloat16)
        .at[jnp.where(filled, slot_token, local_len)]
        .set(result_rows, mode="drop")
    )
    return update[None]


def solution(mesh):
    placed = (P("dp", "ctx", "tensor"), P("dp", "ctx"), P(None, None, "tensor"), P("tensor", None))
    return jax.shard_map(
        per_device, mesh=mesh, in_specs=placed, out_specs=P("dp", "ctx", "tensor"), check_vma=False
    )
```

profile of v0, /device:TPU:1, one launch (start us, length us, event | category | flops | bytes accessed | tf_op | source)
XLA Modules:
  0.0 554.3 jit_solution(16296913542401398679)
XLA Ops:
  11.6 16.9 %all-reduce = s32[32]{0:T(128)S(1)} all-reduce(s32[32]{0:T(128)S(1)} %dynamic-update-slice), channel_id=1, replica_groups=mesh['dp'=8,'ctx'=4,'tensor'=4] {'dp','ctx'}, use_global_device_ids=true, to_apply=%add | all-reduce | flops 32 | bytes 256
  33.9 15.5 %scatter_custom_fusion = s32[1024]{0:T(1024)S(1)} fusion(s32[4096]{0:T(1024)S(1)} %bitcast.67, s32[4096]{0:T(1024)S(1)} %iota.52, s32[]{:T(128)} %constant.133.clone.1), kind=kCustom, calls=%fused_computation.99 | custom fusion | bytes 4100 | tf_op jit(solution)/shard_map/scatter | solution.py:67
  52.0 37.8 %scatter_custom_fusion.2 = bf16[1024,640]{1,0:T(8,128)(2,1)} fusion(s32[1024]{0:T(1024)S(1)} %bitcast.71, pred[1024]{0:T(1024)(128)(4,1)S(1)} %iota_compare_fusion.1, bf16[]{:T(256)} %constant.131.clone.1, bf16[4096,640]{1,0:T(8,128)(2,1)} %bitcast.59, s32[1024]{0:T(1024)S(1)} %get-tuple-element.13), kind=kCustom, calls=%fused_computation.37 | custom fusion | flops 655360 | bytes 6559744 | tf_op jit(solution)/shard_map/scatter | solution.py:99
  89.8 12.2 %all-to-all-start = ((bf16[32,32,640]{2,1,0:T(8,128)(2,1)}), bf16[32,32,640]{2,1,0:T(8,128)(2,1)}, u32[]{:S(2)}, u32[]{:S(2)}) async-start(bf16[32,32,640]{2,1,0:T(8,128)(2,1)} %bitcast.60), calls=%async_computation | async-start | bytes 2621440 | tf_op jit(solution)/shard_map/all_to_all | solution.py:47
  107.9 13.0 %all-to-all-done = bf16[32,32,640]{2,1,0:T(8,128)(2,1)} async-done(((bf16[32,32,640]{2,1,0:T(8,128)(2,1)}), bf16[32,32,640]{2,1,0:T(8,128)(2,1)}, u32[]{:S(2)}, u32[]{:S(2)}) %all-to-all-start) | async-done | bytes 1310752 | tf_op jit(solution)/shard_map/all_to_all | solution.py:47
  125.2 13.9 %copy.19 = bf16[2560,3,640]{0,2,1:T(8,128)(2,1)} copy(bf16[2560,3,640]{2,0,1:T(8,128)(2,1)} %param.6) | data formatting | bytes 19660800 | tf_op args[2]
  139.1 21.1 %all-gather.6.cloned.1.call-done = bf16[512,2560]{1,0:T(8,128)(2,1)} async-done(((bf16[512,640]{1,0:T(8,128)(2,1)}), bf16[512,2560]{1,0:T(8,128)(2,1)}) %all-gather.6.cloned.1.call-update) | async-done | bytes 2621456 | tf_op jit(solution)/shard_map/all_gather | solution.py:23
  162.5 9.3 %fusion.7 = f32[512,1920]{1,0:T(8,128)S(1)} fusion(bf16[2560,1920]{0,1:T(8,128)(2,1)} %bitcast.52, bf16[512,2560]{1,0:T(8,128)(2,1)} %all-gather.6.cloned.1.call-done, f32[512]{0:T(512)S(1)} %add_rsqrt_fusion.2), kind=kOutput, calls=%fused_computation.20 | convolution fusion | flops 5037096960 | bytes 16386048 | tf_op jit(solution)/shard_map/dot_general | solution.py:28
  196.1 7.0 %scatter_custom_fusion.3 = bf16[1024,1920]{1,0:T(8,128)(2,1)} fusion(s32[512]{0:T(512)S(1)} %compare_select_fusion.15, bf16[512,640]{1,0:T(8,128)(2,1)} %slice.81, bf16[]{:T(256)} %constant.171, bf16[512,640]{1,0:T(8,128)(2,1)} %get-tuple-element.10, bf16[512,640]{1,0:T(8,128)(2,1)} %get-tuple-element.9, bf16[]{:T(256)} %constant.131.clone.1), kind=kCustom, calls=%fused_computation.26 | custom fusion | flops 5898240 | bytes 5898244 | tf_op jit(solution)/shard_map/scatter | solution.py:102
  203.1 7.7 %all-to-all-start.1 = ((bf16[32,32,1920]{2,1,0:T(8,128)(2,1)}), bf16[32,32,1920]{2,1,0:T(8,128)(2,1)}, u32[]{:S(2)}, u32[]{:S(2)}) async-start(bf16[32,32,1920]{2,1,0:T(8,128)(2,1)} %bitcast.51), calls=%async_computation.1 | async-start | bytes 7864320 | tf_op jit(solution)/shard_map/all_to_all | solution.py:47
  210.9 47.3 %all-to-all-done.1 = bf16[32,32,1920]{2,1,0:T(8,128)(2,1)} async-done(((bf16[32,32,1920]{2,1,0:T(8,128)(2,1)}), bf16[32,32,1920]{2,1,0:T(8,128)(2,1)}, u32[]{:S(2)}, u32[]{:S(2)}) %all-to-all-start.1) | async-done | bytes 3932192 | tf_op jit(solution)/shard_map/all_to_all | solution.py:47
  258.2 11.1 %gather_fusion.1 = bf16[1024,1920]{1,0:T(8,128)(2,1)} fusion(bf16[1024,1920]{1,0:T(8,128)(2,1)} %bitcast.20, s32[1024]{0:T(1024)S(1)} %broadcast_clamp_fusion.1), kind=kCustom, calls=%fused_computation.2 | custom fusion | bytes 7868416 | tf_op jit(solution)/shard_map/gather | solution.py:103
  272.8 16.7 %gather_fusion.2 = s32[4096]{0:T(1024)S(1)} fusion(s32[1024]{0:T(1024)S(1)} %scatter_custom_fusion, s32[4096]{0:T(1024)S(1)} %broadcast_clamp_fusion), kind=kCustom, calls=%fused_computation.3 | custom fusion | bytes 49152 | tf_op jit(solution)/shard_map/gather | solution.py:115
  293.3 6.2 %and_and_fusion = pred[1024,4096]{1,0:T(8,128)(4,1)} fusion(s32[4096]{0:T(1024)S(1)} %gather_fusion.2, s32[1024]{0:T(1024)S(1)} %scatter_custom_fusion, pred[1024]{0:T(1024)(128)(4,1)S(1)} %iota_compare_fusion.1, pred[4096]{0:T(1024)(128)(4,1)S(1)} %fusion.32, pred[4096]{0:T(1024)(128)(4,1)S(1)} %get-tuple-element.23, pred[4096]{0:T(1024)(128)(4,1)S(1)} %get-tuple-element.24), kind=kLoop, calls=%fused_computation.14 | loop fusion | flops 20971520 | bytes 4228096 | tf_op jit(solution)/shard_map/and | solution.py:118
  304.5 69.3 %all-gather.4.cloned.1.call-done = bf16[4096,1280]{1,0:T(8,128)(2,1)} async-done(((bf16[1024,1280]{1,0:T(8,128)(2,1)}), bf16[4096,1280]{1,0:T(8,128)(2,1)}) %all-gather.4.cloned.1.call-update) | async-done | bytes 10485776 | tf_op jit(solution)/shard_map/all_gather | solution.py:107
  373.8 9.0 %fusion.46 = (bf16[4096,640]{1,0:T(8,128)(2,1)}, bf16[4096,640]{1,0:T(8,128)(2,1)}) fusion(bf16[4096,1280]{1,0:T(8,128)(2,1)} %all-gather.4.cloned.1.call-done), kind=kLoop, calls=%fused_computation.116 | loop fusion | bytes 20971520 | tf_op jit(solution)/shard_map/slice | solution.py:119
  382.8 7.9 %copy.24 = bf16[4096,640]{0,1:T(8,128)(2,1)} copy(bf16[4096,640]{1,0:T(8,128)(2,1)} %get-tuple-element.8) | data formatting | bytes 10485760 | tf_op jit(solution)/shard_map/slice | solution.py:120
  390.8 8.0 %copy.26 = bf16[4096,640]{0,1:T(8,128)(2,1)} copy(bf16[4096,640]{1,0:T(8,128)(2,1)} %get-tuple-element.7) | data formatting | bytes 10485760 | tf_op jit(solution)/shard_map/slice | solution.py:119
  398.8 36.3 %fusion = (f32[5,1024]{1,0:T(8,128)S(1)}, f32[5,1024,4096]{2,1,0:T(8,128)}) fusion(pred[1024,4096]{1,0:T(8,128)(4,1)} %and_and_fusion, bf16[1024,5,128]{0,2,1:T(8,128)(2,1)} %bitcast.61, bf16[4096,5,128]{0,2,1:T(8,128)(2,1)} %bitcast.54), kind=kOutput, calls=%fused_computation.10 | convolution fusion | flops 5431618560 | bytes 94654464 | tf_op jit(solution)/shard_map/qhd,khd->hqk/dot_general | solution.py:122
  435.1 30.0 %fusion.9 = bf16[1024,5,128]{0,2,1:T(8,128)(2,1)S(1)} fusion(bf16[4096,5,128]{0,2,1:T(8,128)(2,1)} %bitcast.53, f32[5,1024,4096]{2,1,0:T(8,128)} %get-tuple-element.20, pred[1024,4096]{1,0:T(8,128)(4,1)} %and_and_fusion, f32[1024,5]{0,1:T(8,128)S(1)} %add_bitcast_fusion), kind=kOutput, calls=%fused_computation.22 | convolution fusion | flops 5432934400 | bytes 94654464 | tf_op jit(solution)/shard_map/hqk,khd->qhd/dot_general | solution.py:126
  465.1 6.3 %convolution_convert_fusion = bf16[1024,2560]{1,0:T(8,128)(2,1)} fusion(bf16[1024,640]{0,1:T(8,128)(2,1)S(1)} %bitcast.73, bf16[640,2560]{1,0:T(8,128)(2,1)S(1)} %copy-done), kind=kOutput, calls=%fused_computation.17 | convolution fusion | flops 3358064640 | bytes 9830400 | tf_op jit(solution)/shard_map/dot_general | solution.py:40
  471.4 8.0 %copy.31 = bf16[1024,2560]{0,1:T(8,128)(2,1)} copy(bf16[1024,2560]{1,0:T(8,128)(2,1)} %convolution_convert_fusion) | data formatting | bytes 10485760
  479.4 56.8 %reduce-scatter.4.cloned.1.call-done = bf16[640,1024]{1,0:T(8,128)(2,1)} async-done(((bf16[2560,1024]{1,0:T(8,128)(2,1)}), bf16[640,1024]{1,0:T(8,128)(2,1)}) %reduce-scatter.4.cloned.1.call-update) | async-done | bytes 1310736
  538.6 9.0 %scatter_custom_fusion.4 = bf16[4096,640]{1,0:T(8,128)(2,1)} fusion(s32[1024]{0:T(1024)} %get-tuple-element.14, bf16[1024,640]{1,0:T(8,128)(2,1)} %copy.32, bf16[]{:T(256)} %constant.131.clone.1), kind=kCustom, calls=%fused_computation.24 | custom fusion | bytes 5243392 | tf_op jit(solution)/shard_map/scatter | solution.py:144
  (78 shorter events, 61.9 us)
Async XLA Ops:
  6.5 458.6 %copy-start = (bf16[640,2560]{1,0:T(8,128)(2,1)S(1)}, bf16[640,2560]{1,0:T(8,128)(2,1)}, u32[]{:S(2)}) copy-start(bf16[640,2560]{1,0:T(8,128)(2,1)} %param.7) | copy-start | bytes 9830404
  89.8 31.1 %all-to-all-start = ((bf16[32,32,640]{2,1,0:T(8,128)(2,1)}), bf16[32,32,640]{2,1,0:T(8,128)(2,1)}, u32[]{:S(2)}, u32[]{:S(2)}) async-start(bf16[32,32,640]{2,1,0:T(8,128)(2,1)} %bitcast.60), calls=%async_computation | async-start | bytes 2621440 | tf_op jit(solution)/shard_map/all_to_all | solution.py:47
  102.0 58.2 %all-gather.6.cloned.1.call-start = ((), (), s32[]{:S(2)}) async-start(), calls=%async_computation.4 | async-start | bytes 3276800 | tf_op jit(solution)/shard_map/all_gather | solution.py:23
  171.8 2.1 copy-start.1
  203.1 55.1 %all-to-all-start.1 = ((bf16[32,32,1920]{2,1,0:T(8,128)(2,1)}), bf16[32,32,1920]{2,1,0:T(8,128)(2,1)}, u32[]{:S(2)}, u32[]{:S(2)}) async-start(bf16[32,32,1920]{2,1,0:T(8,128)(2,1)} %bitcast.51), calls=%async_computation.1 | async-start | bytes 7864320 | tf_op jit(solution)/shard_map/all_to_all | solution.py:47
  210.8 163.0 %all-gather.4.cloned.1.call-start = ((), (), s32[]{:S(2)}) async-start(), calls=%async_computation.3 | async-start | bytes 13107200 | tf_op jit(solution)/shard_map/all_gather | solution.py:107
  272.7 263.4 %reduce-scatter.4.cloned.1.call-start = ((), (), s32[]{:S(2)}) async-start(), calls=%async_computation.5 | async-start | bytes 6553600
Sparse Core Ops, SparseCore 0:
  125.4 34.7 all-gather.5
  272.9 100.8 all-gather.3
  479.5 56.6 reduce-scatter.3
where the time goes:
time: 563 us; the launch traced here: 554 us
  waiting for transfers between devices  208 us (37%)
  local copies, waits for them, and re-layouts  140 us (25%)
  matrix products  81.8 us (15%)
  other arithmetic  72.3 us (13%)
  starting transfers between devices  20 us (4%)
  blocking collectives  16.9 us (3%)
  between operations  16.2 us (3%)
    all_gather x1, waiting for transfers between devices, per_device(): key_piece = lax.all_gather(key_values, 'ctx', axis=0, tiled=True)  69.3 us
    all_to_all x2, waiting for transfers between devices, move_tiles(): lax.all_to_all(payload, ('dp', 'ctx'), split_axis=0, concat_axis=0, tiled...  60.3 us
    unnamed x4, waiting for transfers between devices  56.9 us
    scatter x1, other arithmetic, per_device(): packed = jnp.zeros((capacity,) + token_rows.shape[1:], token_rows.dtype)....  37.8 us
    dot_general x1, matrix products, per_device(): jnp.einsum('qhd,khd->hqk', query_heads, key_heads, preferred_element_type...  36.3 us
    dot_general x1, matrix products, per_device(): jnp.einsum('hqk,khd->qhd', weights.astype(jnp.bfloat16), value_heads, pre...  30 us
    unnamed x10, local copies, waits for them, and re-layouts  28 us
    all_gather x1, waiting for transfers between devices, project_rows(): full_rows = lax.all_gather(token_rows, 'tensor', axis=1, tiled=True)  21.1 us
  transfers between devices with their start and end apart: 5, of which 5 were waited for; matrix products, arithmetic and copies ran while one was open for 9% of the time, Pallas kernels for 0%

commit v1 on v0

--- a/solution.py
+++ b/solution.py
@@ -10,6 +10,16 @@
 score_scale = 0.25
 norm_epsilon = 1e-05
 head_epsilon = 1e-06
+
+
+def around_the_ring(x, axis, along):
+    size = lax.axis_size(axis)
+    current, pieces = (x, [x])
+    for _ in range(size - 1):
+        current = lax.ppermute(current, axis, [(i, (i + 1) % size) for i in range(size)])
+        pieces.insert(0, current)
+    line = jnp.concatenate(pieces, axis=along)
+    return jnp.roll(line, (lax.axis_index(axis) + 1) * x.shape[along], axis=along)
 
 
 def head_normed(values):
@@ -104,7 +114,7 @@
     queries = projected[:, :head_width]
     key_values = projected[:, head_width:]
     query_heads = queries.reshape(capacity, heads_here, HD)
-    key_piece = lax.all_gather(key_values, "ctx", axis=0, tiled=True)
+    key_piece = around_the_ring(key_values, "ctx", 0)
     piece_rows = key_piece.shape[0]
     row_index = jnp.arange(piece_rows, dtype=jnp.int32)
     source_shard = row_index // capacity

time: 563 us -> 659 us (1.17)
  waiting for transfers between devices: 208 us -> 279 us
  local copies, waits for them, and re-layouts: 140 us -> 161 us
    ppermute x0 -> x3, waiting for transfers between devices: none -> 143 us  [around_the_ring(): lax.ppermute(current, axis, [(i, (i + 1) % size) for i in range(size)])]
    all_gather x1 -> x0, waiting for transfers between devices: 69.3 us -> none  [per_device(): key_piece = lax.all_gather(key_values, 'ctx', axis=0, tiled=True)]
    unnamed x10 -> x23, local copies, waits for them, and re-layouts: 28 us -> 49.8 us
    unnamed x4 -> x3, waiting for transfers between devices: 56.9 us -> 54.9 us
  transfers between devices with their start and end apart: 5 -> 7, of which waited for: 5 -> 7; matrix products, arithmetic and copies ran while one was open for 9% -> 8% of each run, Pallas kernels for 0% -> 0%
where the time goes in v1:
time: 659 us; the launch traced here: 650 us
  waiting for transfers between devices  279 us (42%)
  local copies, waits for them, and re-layouts  161 us (24%)
  matrix products  81.9 us (12%)
  other arithmetic  72.4 us (11%)
  starting transfers between devices  21.3 us (3%)
  blocking collectives  16.9 us (3%)
  between operations  16.7 us (3%)
    ppermute x3, waiting for transfers between devices, around_the_ring(): lax.ppermute(current, axis, [(i, (i + 1) % size) for i in range(size)])  143 us
    all_to_all x2, waiting for transfers between devices, move_tiles(): lax.all_to_all(payload, ('dp', 'ctx'), split_axis=0, concat_axis=0, tiled...  60.6 us
    unnamed x3, waiting for transfers between devices  54.9 us
    unnamed x23, local copies, waits for them, and re-layouts  49.8 us
    scatter x1, other arithmetic, per_device(): packed = jnp.zeros((capacity,) + token_rows.shape[1:], token_rows.dtype)....  37.8 us
    dot_general x1, matrix products, per_device(): jnp.einsum('qhd,khd->hqk', query_heads, key_heads, preferred_element_type...  36.3 us
    dot_general x1, matrix products, per_device(): jnp.einsum('hqk,khd->qhd', weights.astype(jnp.bfloat16), value_heads, pre...  30.2 us
    all_gather x1, waiting for transfers between devices, project_rows(): full_rows = lax.all_gather(token_rows, 'tensor', axis=1, tiled=True)  21.1 us
  transfers between devices with their start and end apart: 7, of which 7 were waited for; matrix products, arithmetic and copies ran while one was open for 8% of the time, Pallas kernels for 0%

profile of v1, /device:TPU:1, one launch (start us, length us, event | category | flops | bytes accessed | tf_op | source)
XLA Modules:
  0.0 649.6 jit_solution(13747589565638169358)
XLA Ops:
  11.5 16.9 %all-reduce = s32[32]{0:T(128)S(1)} all-reduce(s32[32]{0:T(128)S(1)} %dynamic-update-slice), channel_id=1, replica_groups=mesh['dp'=8,'ctx'=4,'tensor'=4] {'dp','ctx'}, use_global_device_ids=true, to_apply=%add | all-reduce | flops 32 | bytes 256
  33.9 15.5 %scatter_custom_fusion = s32[1024]{0:T(1024)S(1)} fusion(s32[4096]{0:T(1024)S(1)} %bitcast.67, s32[4096]{0:T(1024)S(1)} %iota.52, s32[]{:T(128)} %constant.152.clone.1), kind=kCustom, calls=%fused_computation.107 | custom fusion | bytes 4100 | tf_op jit(solution)/shard_map/scatter | solution.py:77
  52.0 37.8 %scatter_custom_fusion.2 = bf16[1024,640]{1,0:T(8,128)(2,1)} fusion(s32[1024]{0:T(1024)S(1)} %bitcast.71, pred[1024]{0:T(1024)(128)(4,1)S(1)} %iota_compare_fusion.1, bf16[]{:T(256)} %constant.150.clone.1, bf16[4096,640]{1,0:T(8,128)(2,1)} %bitcast.59, s32[1024]{0:T(1024)S(1)} %get-tuple-element.13), kind=kCustom, calls=%fused_computation.37 | custom fusion | flops 655360 | bytes 6559744 | tf_op jit(solution)/shard_map/scatter | solution.py:109
  89.8 12.2 %all-to-all-start = ((bf16[32,32,640]{2,1,0:T(8,128)(2,1)}), bf16[32,32,640]{2,1,0:T(8,128)(2,1)}, u32[]{:S(2)}, u32[]{:S(2)}) async-start(bf16[32,32,640]{2,1,0:T(8,128)(2,1)} %bitcast.60), calls=%async_computation | async-start | bytes 2621440 | tf_op jit(solution)/shard_map/all_to_all | solution.py:57
  107.6 13.3 %all-to-all-done = bf16[32,32,640]{2,1,0:T(8,128)(2,1)} async-done(((bf16[32,32,640]{2,1,0:T(8,128)(2,1)}), bf16[32,32,640]{2,1,0:T(8,128)(2,1)}, u32[]{:S(2)}, u32[]{:S(2)}) %all-to-all-start) | async-done | bytes 1310752 | tf_op jit(solution)/shard_map/all_to_all | solution.py:57
  125.3 13.9 %copy.19 = bf16[2560,3,640]{0,2,1:T(8,128)(2,1)} copy(bf16[2560,3,640]{2,0,1:T(8,128)(2,1)} %param.6) | data formatting | bytes 19660800 | tf_op args[2]
  139.1 21.1 %all-gather.3.cloned.1.call-done = bf16[512,2560]{1,0:T(8,128)(2,1)} async-done(((bf16[512,640]{1,0:T(8,128)(2,1)}), bf16[512,2560]{1,0:T(8,128)(2,1)}) %all-gather.3.cloned.1.call-update) | async-done | bytes 2621456 | tf_op jit(solution)/shard_map/all_gather | solution.py:33
  162.5 9.3 %fusion.7 = f32[512,1920]{1,0:T(8,128)S(1)} fusion(bf16[2560,1920]{0,1:T(8,128)(2,1)} %bitcast.52, bf16[512,2560]{1,0:T(8,128)(2,1)} %all-gather.3.cloned.1.call-done, f32[512]{0:T(512)S(1)} %add_rsqrt_fusion.2), kind=kOutput, calls=%fused_computation.20 | convolution fusion | flops 5037096960 | bytes 16386048 | tf_op jit(solution)/shard_map/dot_general | solution.py:38
  196.1 7.0 %scatter_custom_fusion.3 = bf16[1024,1920]{1,0:T(8,128)(2,1)} fusion(s32[512]{0:T(512)S(1)} %compare_select_fusion.15, bf16[512,640]{1,0:T(8,128)(2,1)} %slice.81, bf16[]{:T(256)} %constant.200, bf16[512,640]{1,0:T(8,128)(2,1)} %get-tuple-element.10, bf16[512,640]{1,0:T(8,128)(2,1)} %get-tuple-element.9, bf16[]{:T(256)} %constant.150.clone.1), kind=kCustom, calls=%fused_computation.26 | custom fusion | flops 5898240 | bytes 5898244 | tf_op jit(solution)/shard_map/scatter | solution.py:112
  203.1 7.8 %all-to-all-start.1 = ((bf16[32,32,1920]{2,1,0:T(8,128)(2,1)}), bf16[32,32,1920]{2,1,0:T(8,128)(2,1)}, u32[]{:S(2)}, u32[]{:S(2)}) async-start(bf16[32,32,1920]{2,1,0:T(8,128)(2,1)} %bitcast.51), calls=%async_computation.1 | async-start | bytes 7864320 | tf_op jit(solution)/shard_map/all_to_all | solution.py:57
  210.9 47.3 %all-to-all-done.1 = bf16[32,32,1920]{2,1,0:T(8,128)(2,1)} async-done(((bf16[32,32,1920]{2,1,0:T(8,128)(2,1)}), bf16[32,32,1920]{2,1,0:T(8,128)(2,1)}, u32[]{:S(2)}, u32[]{:S(2)}) %all-to-all-start.1) | async-done | bytes 3932192 | tf_op jit(solution)/shard_map/all_to_all | solution.py:57
  258.2 11.1 %gather_fusion.1 = bf16[1024,1920]{1,0:T(8,128)(2,1)} fusion(bf16[1024,1920]{1,0:T(8,128)(2,1)} %bitcast.20, s32[1024]{0:T(1024)S(1)} %broadcast_clamp_fusion.1), kind=kCustom, calls=%fused_computation.2 | custom fusion | bytes 7868416 | tf_op jit(solution)/shard_map/gather | solution.py:113
  272.5 58.8 %collective-permute-done = bf16[1024,1280]{1,0:T(8,128)(2,1)S(1)} collective-permute-done((bf16[1024,1280]{1,0:T(8,128)(2,1)S(1)}, bf16[1024,1280]{1,0:T(8,128)(2,1)S(1)}, u32[]{:S(2)}, u32[]{:S(2)}) %collective-permute-start) | collective-permute-done | bytes 2621472 | tf_op jit(solution)/shard_map/ppermute | solution.py:19
  332.8 58.2 %collective-permute-done.1 = bf16[1024,1280]{1,0:T(8,128)(2,1)} collective-permute-done((bf16[1024,1280]{1,0:T(8,128)(2,1)S(1)}, bf16[1024,1280]{1,0:T(8,128)(2,1)}, u32[]{:S(2)}, u32[]{:S(2)}) %collective-permute-start.1) | collective-permute-done | bytes 2621472 | tf_op jit(solution)/shard_map/ppermute | solution.py:19
  391.1 16.7 %gather_fusion.2 = s32[4096]{0:T(1024)S(1)} fusion(s32[1024]{0:T(1024)S(1)} %scatter_custom_fusion, s32[4096]{0:T(1024)S(1)} %broadcast_clamp_fusion), kind=kCustom, calls=%fused_computation.3 | custom fusion | bytes 49152 | tf_op jit(solution)/shard_map/gather | solution.py:125
  422.9 25.7 %collective-permute-done.2 = bf16[1024,1280]{1,0:T(8,128)(2,1)} collective-permute-done((bf16[1024,1280]{1,0:T(8,128)(2,1)}, bf16[1024,1280]{1,0:T(8,128)(2,1)}, u32[]{:S(2)}, u32[]{:S(2)}) %collective-permute-start.2) | collective-permute-done | bytes 2621472 | tf_op jit(solution)/shard_map/ppermute | solution.py:19
  470.4 9.0 %constant_dynamic-slice_fusion = (bf16[4096,640]{1,0:T(8,128)(2,1)}, bf16[4096,640]{1,0:T(8,128)(2,1)}) fusion(bf16[8192,1280]{1,0:T(8,128)(2,1)} %constant_dynamic-update-slice_fusion, s32[]{:T(128)S(6)} %select_n.243, s32[]{:T(128)S(6)} %add.286), kind=kLoop, calls=%fused_computation.120 | loop fusion | bytes 20971528 | tf_op jit(solution)/shard_map/slice | solution.py:129
  479.4 7.9 %copy.24 = bf16[4096,640]{0,1:T(8,128)(2,1)} copy(bf16[4096,640]{1,0:T(8,128)(2,1)} %get-tuple-element.8) | data formatting | bytes 10485760 | tf_op jit(solution)/shard_map/slice | solution.py:130
  487.4 8.0 %copy.26 = bf16[4096,640]{0,1:T(8,128)(2,1)} copy(bf16[4096,640]{1,0:T(8,128)(2,1)} %get-tuple-element.7) | data formatting | bytes 10485760 | tf_op jit(solution)/shard_map/slice | solution.py:129
  495.4 36.3 %fusion = (f32[5,1024]{1,0:T(8,128)S(1)}, f32[5,1024,4096]{2,1,0:T(8,128)}) fusion(pred[1024,4096]{1,0:T(8,128)(4,1)} %and_and_fusion, bf16[1024,5,128]{0,2,1:T(8,128)(2,1)} %bitcast.61, bf16[4096,5,128]{0,2,1:T(8,128)(2,1)} %bitcast.54), kind=kOutput, calls=%fused_computation.10 | convolution fusion | flops 5431618560 | bytes 94654464 | tf_op jit(solution)/shard_map/qhd,khd->hqk/dot_general | solution.py:132
  531.7 30.2 %fusion.9 = bf16[1024,5,128]{0,2,1:T(8,128)(2,1)S(1)} fusion(bf16[4096,5,128]{0,2,1:T(8,128)(2,1)} %bitcast.53, f32[5,1024,4096]{2,1,0:T(8,128)} %get-tuple-element.20, pred[1024,4096]{1,0:T(8,128)(4,1)} %and_and_fusion, f32[1024,5]{0,1:T(8,128)S(1)} %add_bitcast_fusion), kind=kOutput, calls=%fused_computation.22 | convolution fusion | flops 5432934400 | bytes 94654464 | tf_op jit(solution)/shard_map/hqk,khd->qhd/dot_general | solution.py:136
  568.0 8.0 %copy.31 = bf16[1024,2560]{0,1:T(8,128)(2,1)} copy(bf16[1024,2560]{1,0:T(8,128)(2,1)} %convolution_convert_fusion) | data formatting | bytes 10485760
  576.0 54.9 %reduce-scatter.4.cloned.1.call-done = bf16[640,1024]{1,0:T(8,128)(2,1)} async-done(((bf16[2560,1024]{1,0:T(8,128)(2,1)}), bf16[640,1024]{1,0:T(8,128)(2,1)}) %reduce-scatter.4.cloned.1.call-update) | async-done | bytes 1310736
  633.3 9.0 %scatter_custom_fusion.4 = bf16[4096,640]{1,0:T(8,128)(2,1)} fusion(s32[1024]{0:T(1024)} %get-tuple-element.14, bf16[1024,640]{1,0:T(8,128)(2,1)} %copy.32, bf16[]{:T(256)} %constant.150.clone.1), kind=kCustom, calls=%fused_computation.24 | custom fusion | bytes 5243392 | tf_op jit(solution)/shard_map/scatter | solution.py:154
  (95 shorter events, 97.1 us)
Async XLA Ops:
  6.5 555.4 %copy-start = (bf16[640,2560]{1,0:T(8,128)(2,1)S(1)}, bf16[640,2560]{1,0:T(8,128)(2,1)}, u32[]{:S(2)}) copy-start(bf16[640,2560]{1,0:T(8,128)(2,1)} %param.7) | copy-start | bytes 9830404
  89.8 31.1 %all-to-all-start = ((bf16[32,32,640]{2,1,0:T(8,128)(2,1)}), bf16[32,32,640]{2,1,0:T(8,128)(2,1)}, u32[]{:S(2)}, u32[]{:S(2)}) async-start(bf16[32,32,640]{2,1,0:T(8,128)(2,1)} %bitcast.60), calls=%async_computation | async-start | bytes 2621440 | tf_op jit(solution)/shard_map/all_to_all | solution.py:57
  102.0 58.2 %all-gather.3.cloned.1.call-start = ((), (), s32[]{:S(2)}) async-start(), calls=%async_computation.3 | async-start | bytes 3276800 | tf_op jit(solution)/shard_map/all_gather | solution.py:33
  171.8 2.1 copy-start.4
  203.1 55.2 %all-to-all-start.1 = ((bf16[32,32,1920]{2,1,0:T(8,128)(2,1)}), bf16[32,32,1920]{2,1,0:T(8,128)(2,1)}, u32[]{:S(2)}, u32[]{:S(2)}) async-start(bf16[32,32,1920]{2,1,0:T(8,128)(2,1)} %bitcast.51), calls=%async_computation.1 | async-start | bytes 7864320 | tf_op jit(solution)/shard_map/all_to_all | solution.py:57
  210.9 420.0 %reduce-scatter.4.cloned.1.call-start = ((), (), s32[]{:S(2)}) async-start(), calls=%async_computation.4 | async-start | bytes 6553600
  271.2 60.1 %collective-permute-start = (bf16[1024,1280]{1,0:T(8,128)(2,1)S(1)}, bf16[1024,1280]{1,0:T(8,128)(2,1)S(1)}, u32[]{:S(2)}, u32[]{:S(2)}) collective-permute-start(bf16[1024,1280]{1,0:T(8,128)(2,1)S(1)} %slice.66), channel_id=1, source_target_pairs={{0,4},{4,8},{8,12},{12,0},{1,5},{5,9},{9,13},{13,1},{2,6},{6,10},{... | collective-permute-start | bytes 7864328 | tf_op jit(solution)/shard_map/ppermute | solution.py:19
  331.3 1.5 copy-start.2
  332.8 58.2 %collective-permute-start.1 = (bf16[1024,1280]{1,0:T(8,128)(2,1)S(1)}, bf16[1024,1280]{1,0:T(8,128)(2,1)}, u32[]{:S(2)}, u32[]{:S(2)}) collective-permute-start(bf16[1024,1280]{1,0:T(8,128)(2,1)S(1)} %collective-permute-done), channel_id=1, source_target_pairs={{0,4},{4,8},{8,12},{12,0},{1,5},{5,9},{9,13},{13,1},{2,6},{6,10},{... | collective-permute-start | bytes 7864328 | tf_op jit(solution)/shard_map/ppermute | solution.py:19
  391.0 57.5 %collective-permute-start.2 = (bf16[1024,1280]{1,0:T(8,128)(2,1)}, bf16[1024,1280]{1,0:T(8,128)(2,1)}, u32[]{:S(2)}, u32[]{:S(2)}) collective-permute-start(bf16[1024,1280]{1,0:T(8,128)(2,1)} %collective-permute-done.1), channel_id=1, source_target_pairs={{0,4},{4,8},{8,12},{12,0},{1,5},{5,9},{9,13},{13,1},{2,6},{6,10},{... | collective-permute-start | bytes 7864328 | tf_op jit(solution)/shard_map/ppermute | solution.py:19
  452.0 3.6 copy-start.3
  455.6 3.1 copy-start.1
Sparse Core Ops, SparseCore 0:
  125.4 34.7 all-gather.2
  576.1 54.7 reduce-scatter.3
